TPU v7x, 32 devices: a whole 2x2x4 slice. The times are simulated.
32 devices in a mesh: wide: 8 (over z, x), ffn: 4 (over y, core).
Axes of the slice: x: 2, y: 2, z: 4, core: 2. Of those that a mesh axis runs over, the one named last changes fastest.
Arguments:
- hidden_in: bfloat16 [8192, 1024], P(('wide', 'ffn')), may hold values from -6 to 6
- doc_ids: int32 [8192], P(('wide', 'ffn')), may hold values from -1 to 3, as said below
- out_grad: bfloat16 [8192, 1024], P(('wide', 'ffn')), may hold values from -6 to 6
- w_query: bfloat16 [1024, 1024], P(('wide', 'ffn')), may hold values from -0.25 to 0.25
- b_query: bfloat16 [1024], P(('wide', 'ffn')), may hold values from -1.1953125 to 1.1953125
- w_key: bfloat16 [1024, 1024], P(('wide', 'ffn')), may hold values from -0.25 to 0.25
- w_value: bfloat16 [1024, 1024], P(('wide', 'ffn')), may hold values from -0.1875 to 0.1875
- b_value: bfloat16 [1024], P(('wide', 'ffn')), may hold values from -1.1953125 to 1.1953125
- w_output: bfloat16 [1024, 1024], P(('wide', 'ffn')), may hold values from -0.75 to 0.75
- b_output: bfloat16 [1024], P(('wide', 'ffn')), may hold values from -1.1953125 to 1.1953125
- attn_gain: bfloat16 [1024], P(('wide', 'ffn')), may hold values from 0.25 to 1.75
- attn_shift: bfloat16 [1024], P(('wide', 'ffn')), may hold values from -1.1953125 to 1.1953125
- w_up: bfloat16 [1024, 4096], P('wide', 'ffn'), may hold values from -0.1875 to 0.1875
- b_up: bfloat16 [4096], P(('wide', 'ffn')), may hold values from -1.1953125 to 1.1953125
- w_down: bfloat16 [4096, 1024], P('ffn', 'wide'), may hold values from -0.09375 to 0.09375
- b_down: bfloat16 [1024], P(('wide', 'ffn')), may hold values from -1.1953125 to 1.1953125
- ffn_gain: bfloat16 [1024], P(('wide', 'ffn')), may hold values from 0.25 to 1.75
- ffn_shift: bfloat16 [1024], P(('wide', 'ffn')), may hold values from -1.1953125 to 1.1953125
Outputs:
- out_rows: bfloat16 [8192, 1024], P(('wide', 'ffn'))
- grad_input: float32 [8192, 1024], P(('wide', 'ffn'))
- grad_w_query: float32 [1024, 1024], P(('wide', 'ffn'))
- grad_b_query: float32 [1024], P(('wide', 'ffn'))
- grad_w_key: float32 [1024, 1024], P(('wide', 'ffn'))
- grad_w_value: float32 [1024, 1024], P(('wide', 'ffn'))
- grad_b_value: float32 [1024], P(('wide', 'ffn'))
- grad_w_output: float32 [1024, 1024], P(('wide', 'ffn'))
- grad_b_output: float32 [1024], P(('wide', 'ffn'))
- grad_attn_gain: float32 [1024], P(('wide', 'ffn'))
- grad_attn_shift: float32 [1024], P(('wide', 'ffn'))
- grad_w_up: float32 [1024, 4096], P('wide', 'ffn')
- grad_b_up: float32 [4096], P(('wide', 'ffn'))
- grad_w_down: float32 [4096, 1024], P('ffn', 'wide')
- grad_b_down: float32 [1024], P(('wide', 'ffn'))
- grad_ffn_gain: float32 [1024], P(('wide', 'ffn'))
- grad_ffn_shift: float32 [1024], P(('wide', 'ffn'))
Inputs may be any that keep to these rules, and one draw needn't show every extreme that they name: `doc_ids`: within each device's 256 rows either all rows are item 0 (one item of 256 residues), or items 0 to c - 1 of 64 residues each fill the first c * 64 rows for some c of 1 to 4 and the remaining rows are -1. In every draw some device holds one full item and some device holds four short ones.
All inputs are finite; a program needn't handle non-finite values.
Results may differ from a plain program's by a relative error of at most 0.015.
The roundings to bfloat16 on the way count: a program that leaves them out, or rounds other values in their place, can miss the bound.
Values may be sent and summed in bfloat16 or wider, within the bound.
No kernel may reach another device: no remote copies, remote signals or barrier semaphores. Data moves between devices by JAX's collectives and lax.ppermute only.
A program may use at most 128 MiB of HBM per device.

v0:
```python
import math
import jax
import jax.numpy as jnp
from jax import lax
from jax.sharding import PartitionSpec as P

D = 1024
HEADS = 16
HEAD_DIM = 64
norm_eps = 1e-12


def matmul(left, right):
    return jnp.dot(left, right, preferred_element_type=jnp.float32)


def matmul_tn(left, right):
    return lax.dot_general(
        left, right, (((0,), (0,)), ((), ())), preferred_element_type=jnp.float32
    )


def matmul_nt(left, right):
    return lax.dot_general(
        left, right, (((1,), (1,)), ((), ())), preferred_element_type=jnp.float32
    )


def layer_norm(values, gain, shift):
    centre = values - jnp.mean(values, axis=-1, keepdims=True)
    inverse = lax.rsqrt(jnp.mean(centre * centre, axis=-1, keepdims=True) + norm_eps)
    normed = centre * inverse
    return (normed * gain + shift, normed, inverse)


def norm_back(grad, normed, inverse):
    return inverse * (
        grad
        - jnp.mean(grad, axis=-1, keepdims=True)
        - normed * jnp.mean(grad * normed, axis=-1, keepdims=True)
    )


def gelu_exact(values):
    return 0.5 * values * (1.0 + jax.scipy.special.erf(values * (1.0 / math.sqrt(2.0))))


def gelu_slope(values):
    return 0.5 * (1.0 + jax.scipy.special.erf(values * (1.0 / math.sqrt(2.0)))) + values * jnp.exp(
        -0.5 * values * values
    ) * (1.0 / math.sqrt(2.0 * math.pi))


def masked_scores(queries, key_rows, allowed, score_scale):
    scores = (
        jnp.einsum("qhd,khd->hqk", queries, key_rows, preferred_element_type=jnp.float32)
        * score_scale
    )
    return jnp.where(allowed[None, :, :], scores, -1000000000.0)


def column_sum(values):
    return jnp.sum(values.astype(jnp.float32), axis=0)


def body(
    hidden_in,
    doc_ids,
    out_grad,
    w_query,
    b_query,
    w_key,
    w_value,
    b_value,
    w_output,
    b_output,
    attn_gain,
    attn_shift,
    w_up,
    b_up,
    w_down,
    b_down,
    ffn_gain,
    ffn_shift,
):
    gathered = (
        lax.all_gather(w_query, ("wide", "ffn"), axis=0, tiled=True),
        lax.all_gather(w_key, ("wide", "ffn"), axis=0, tiled=True),
        lax.all_gather(w_value, ("wide", "ffn"), axis=0, tiled=True),
        lax.all_gather(w_output, ("wide", "ffn"), axis=0, tiled=True),
        lax.all_gather(b_query, ("wide", "ffn"), axis=0, tiled=True),
        lax.all_gather(b_value, ("wide", "ffn"), axis=0, tiled=True),
        lax.all_gather(b_output, ("wide", "ffn"), axis=0, tiled=True),
        lax.all_gather(attn_gain, ("wide", "ffn"), axis=0, tiled=True),
        lax.all_gather(attn_shift, ("wide", "ffn"), axis=0, tiled=True),
        lax.all_gather(b_up, ("wide", "ffn"), axis=0, tiled=True),
        lax.all_gather(b_down, ("wide", "ffn"), axis=0, tiled=True),
        lax.all_gather(ffn_gain, ("wide", "ffn"), axis=0, tiled=True),
        lax.all_gather(ffn_shift, ("wide", "ffn"), axis=0, tiled=True),
    )
    query_full, key_full, value_full, output_full = (
        gathered[0],
        gathered[1],
        gathered[2],
        gathered[3],
    )
    (
        bias_query,
        bias_value,
        bias_output,
        gain_one,
        shift_one,
        bias_up_all,
        bias_down,
        gain_two,
        shift_two,
    ) = [vector.astype(jnp.float32) for vector in gathered[4:]]
    up_part, down_part = (
        lax.all_gather(w_up, "wide", axis=0, tiled=True),
        lax.all_gather(w_down, "wide", axis=1, tiled=True),
    )
    row_count = hidden_in.shape[0]
    score_scale = HEAD_DIM ** (-0.5)
    residual_in = hidden_in.astype(jnp.float32)
    queries = (
        (matmul(hidden_in, query_full) + bias_query)
        .astype(jnp.bfloat16)
        .reshape(row_count, HEADS, HEAD_DIM)
    )
    key_rows = matmul(hidden_in, key_full).astype(jnp.bfloat16).reshape(row_count, HEADS, HEAD_DIM)
    value_rows = (
        (matmul(hidden_in, value_full) + bias_value)
        .astype(jnp.bfloat16)
        .reshape(row_count, HEADS, HEAD_DIM)
    )
    allowed = doc_ids[:, None] == doc_ids[None, :]
    scores = masked_scores(queries, key_rows, allowed, score_scale)
    top_score = jnp.max(scores, axis=-1, keepdims=True)
    expo_terms = jnp.exp(scores - top_score)
    total_sum = jnp.sum(expo_terms, axis=-1, keepdims=True)
    attn_probs = expo_terms / total_sum
    log_total = top_score + jnp.log(total_sum)
    context = (
        jnp.einsum(
            "hqk,khd->qhd",
            attn_probs.astype(jnp.bfloat16),
            value_rows,
            preferred_element_type=jnp.float32,
        )
        .reshape(row_count, D)
        .astype(jnp.bfloat16)
    )
    attended = matmul(context, output_full) + bias_output
    normed_out, normed_one, inverse_one = layer_norm(residual_in + attended, gain_one, shift_one)
    normed_low = normed_out.astype(jnp.bfloat16)
    slice_len = up_part.shape[1]
    member = lax.axis_index("ffn")
    bias_up = lax.dynamic_slice_in_dim(bias_up_all, member * slice_len, slice_len)
    group_rows = lax.all_gather(normed_low, "ffn", axis=0, tiled=True)
    up_rows = matmul(group_rows, up_part) + bias_up
    active_low = gelu_exact(up_rows).astype(jnp.bfloat16)
    down_rows = (
        lax.psum_scatter(
            matmul(active_low, down_part).astype(jnp.bfloat16),
            "ffn",
            scatter_dimension=0,
            tiled=True,
        ).astype(jnp.float32)
        + bias_down
    )
    layer_out, normed_two, inverse_two = layer_norm(normed_out + down_rows, gain_two, shift_two)
    grad_out = out_grad.astype(jnp.float32)
    grad_gain_two = jnp.sum(grad_out * normed_two, axis=0)
    grad_shift_two = jnp.sum(grad_out, axis=0)
    grad_two = norm_back(grad_out * gain_two, normed_two, inverse_two)
    grad_two_low = grad_two.astype(jnp.bfloat16)
    grad_bias_down = column_sum(grad_two_low)
    grad_group = lax.all_gather(grad_two_low, "ffn", axis=0, tiled=True)
    grad_active = matmul_nt(grad_group, down_part)
    grad_up_low = (grad_active * gelu_slope(up_rows)).astype(jnp.bfloat16)
    grad_bias_up = lax.dynamic_update_slice_in_dim(
        jnp.zeros(bias_up_all.shape, jnp.float32), column_sum(grad_up_low), member * slice_len, 0
    )
    grad_up_w = matmul_tn(group_rows, grad_up_low)
    grad_down_w = matmul_tn(active_low, grad_group)
    grad_one = grad_two + lax.psum_scatter(
        matmul_nt(grad_up_low, up_part).astype(jnp.bfloat16), "ffn", scatter_dimension=0, tiled=True
    ).astype(jnp.float32)
    grad_up_w, grad_down_w = (
        lax.psum_scatter(grad_up_w, "wide", scatter_dimension=0, tiled=True),
        lax.psum_scatter(grad_down_w, "wide", scatter_dimension=1, tiled=True),
    )
    grad_gain_one = jnp.sum(grad_one * normed_one, axis=0)
    grad_shift_one = jnp.sum(grad_one, axis=0)
    grad_z_one = norm_back(grad_one * gain_one, normed_one, inverse_one)
    grad_att_low = grad_z_one.astype(jnp.bfloat16)
    grad_bias_output = column_sum(grad_att_low)
    grad_output_w = matmul_tn(context, grad_att_low)
    grad_context = (
        matmul_nt(grad_att_low, output_full)
        .astype(jnp.bfloat16)
        .reshape(row_count, HEADS, HEAD_DIM)
    )
    scores = masked_scores(queries, key_rows, allowed, score_scale)
    attn_probs = jnp.exp(scores - log_total)
    grad_probs = jnp.einsum(
        "qhd,khd->hqk", grad_context, value_rows, preferred_element_type=jnp.float32
    )
    grad_values = (
        jnp.einsum(
            "hqk,qhd->khd",
            attn_probs.astype(jnp.bfloat16),
            grad_context,
            preferred_element_type=jnp.float32,
        )
        .astype(jnp.bfloat16)
        .reshape(row_count, D)
    )
    row_inner = jnp.sum(attn_probs * grad_probs, axis=-1, keepdims=True)
    grad_scores = (attn_probs * (grad_probs - row_inner)).astype(jnp.bfloat16)
    grad_queries = (
        (
            jnp.einsum("hqk,khd->qhd", grad_scores, key_rows, preferred_element_type=jnp.float32)
            * score_scale
        )
        .astype(jnp.bfloat16)
        .reshape(row_count, D)
    )
    grad_keys = (
        (
            jnp.einsum("hqk,qhd->khd", grad_scores, queries, preferred_element_type=jnp.float32)
            * score_scale
        )
        .astype(jnp.bfloat16)
        .reshape(row_count, D)
    )
    grad_query_w = matmul_tn(hidden_in, grad_queries)
    grad_key_w = matmul_tn(hidden_in, grad_keys)
    grad_value_w = matmul_tn(hidden_in, grad_values)
    grad_input = (
        grad_z_one
        + matmul_nt(grad_queries, query_full)
        + matmul_nt(grad_keys, key_full)
        + matmul_nt(grad_values, value_full)
    )
    summed = (
        lax.psum_scatter(grad_query_w, ("wide", "ffn"), scatter_dimension=0, tiled=True),
        lax.psum_scatter(grad_key_w, ("wide", "ffn"), scatter_dimension=0, tiled=True),
        lax.psum_scatter(grad_value_w, ("wide", "ffn"), scatter_dimension=0, tiled=True),
        lax.psum_scatter(grad_output_w, ("wide", "ffn"), scatter_dimension=0, tiled=True),
        lax.psum_scatter(
            column_sum(grad_queries), ("wide", "ffn"), scatter_dimension=0, tiled=True
        ),
        lax.psum_scatter(column_sum(grad_values), ("wide", "ffn"), scatter_dimension=0, tiled=True),
        lax.psum_scatter(grad_bias_output, ("wide", "ffn"), scatter_dimension=0, tiled=True),
        lax.psum_scatter(grad_gain_one, ("wide", "ffn"), scatter_dimension=0, tiled=True),
        lax.psum_scatter(grad_shift_one, ("wide", "ffn"), scatter_dimension=0, tiled=True),
        lax.psum_scatter(grad_bias_up, ("wide", "ffn"), scatter_dimension=0, tiled=True),
        lax.psum_scatter(grad_bias_down, ("wide", "ffn"), scatter_dimension=0, tiled=True),
        lax.psum_scatter(grad_gain_two, ("wide", "ffn"), scatter_dimension=0, tiled=True),
        lax.psum_scatter(grad_shift_two, ("wide", "ffn"), scatter_dimension=0, tiled=True),
    )
    return (
        layer_out.astype(jnp.bfloat16),
        grad_input,
        summed[0],
        summed[4],
        summed[1],
        summed[2],
        summed[5],
        summed[3],
        summed[6],
        summed[7],
        summed[8],
        grad_up_w,
        summed[9],
        grad_down_w,
        summed[10],
        summed[11],
        summed[12],
    )


def solution(mesh):
    in_specs = (
        P(("wide", "ffn"), None),
        P(("wide", "ffn")),
        P(("wide", "ffn"), None),
        P(("wide", "ffn"), None),
        P(("wide", "ffn")),
        P(("wide", "ffn"), None),
        P(("wide", "ffn"), None),
        P(("wide", "ffn")),
        P(("wide", "ffn"), None),
        P(("wide", "ffn")),
        P(("wide", "ffn")),
        P(("wide", "ffn")),
        P("wide", "ffn"),
        P(("wide", "ffn")),
        P("ffn", "wide"),
        P(("wide", "ffn")),
        P(("wide", "ffn")),
        P(("wide", "ffn")),
    )
    out_specs = (
        P(("wide", "ffn"), None),
        P(("wide", "ffn"), None),
        P(("wide", "ffn"), None),
        P(("wide", "ffn")),
        P(("wide", "ffn"), None),
        P(("wide", "ffn"), None),
        P(("wide", "ffn")),
        P(("wide", "ffn"), None),
        P(("wide", "ffn")),
        P(("wide", "ffn")),
        P(("wide", "ffn")),
        P("wide", "ffn"),
        P(("wide", "ffn")),
        P("ffn", "wide"),
        P(("wide", "ffn")),
        P(("wide", "ffn")),
        P(("wide", "ffn")),
    )
    return jax.shard_map(body, mesh=mesh, in_specs=in_specs, out_specs=out_specs, check_vma=False)
```

profile of v0, /device:TPU:0, one launch (start us, length us, event | category | flops | bytes accessed | tf_op | source)
XLA Modules:
  0.0 1234.9 jit_solution(16796781667847248619)
XLA Ops:
  17.3 42.2 %all-reduce.18 = (bf16[1024]{0:T(1024)(128)(2,1)S(1)}, bf16[1024]{0:T(1024)(128)(2,1)S(1)}, bf16[1024]{0:T(1024)(128)(2,1)S(1)}, bf16[1024]{0:T(1024)(128)(2,1)S...) all-reduce(bf16[1024]{0:T(1024)(128)(2,1)S(1)} %dynamic-update-slic, ...), channel_id=1, replica_groups=mesh['wide'=8,'ffn'=4] {'wide','ffn'}, use_global_device_ids=true, to_apply=%add | all-reduce | flops 8192 | bytes 32768
  60.5 9.6 all-gather.12.cloned.1.call-done
  72.7 55.4 %all-gather.14.cloned.1.call-done = bf16[1024,1024]{1,0:T(8,128)(2,1)} async-done(((bf16[32,1024]{1,0:T(8,128)(2,1)}), bf16[1024,1024]{1,0:T(8,128)(2,1)}) %all-gather.14.cloned.1.call-update) | async-done | bytes 2097168 | tf_op jit(solution)/shard_map/all_gather | solution.py:88
  130.6 55.5 %all-gather.10.cloned.1.call-done = bf16[1024,1024]{1,0:T(8,128)(2,1)} async-done(((bf16[32,1024]{1,0:T(8,128)(2,1)}), bf16[1024,1024]{1,0:T(8,128)(2,1)}) %all-gather.10.cloned.1.call-update) | async-done | bytes 2097168 | tf_op jit(solution)/shard_map/all_gather | solution.py:89
  192.3 51.6 %all-gather.16.cloned.1.call-done = bf16[1024,1024]{1,0:T(8,128)(2,1)} async-done(((bf16[32,1024]{1,0:T(8,128)(2,1)}), bf16[1024,1024]{1,0:T(8,128)(2,1)}) %all-gather.16.cloned.1.call-update) | async-done | bytes 2097168 | tf_op jit(solution)/shard_map/all_gather | solution.py:90
  248.5 39.9 %all-gather = bf16[32,1,128]{2,1,0:T(2,128)(2,1)S(1)} all-gather(bf16[1,1,128]{2,1,0:T(2,128)(2,1)S(1)} %bitcast.90), channel_id=1, replica_groups=mesh['wide'=8,'ffn'=4] {'wide','ffn'}, dimensions={0}, use_global_device_ids=true | all-gather | bytes 8448 | tf_op jit(solution)/shard_map/all_gather | solution.py:96
  288.4 5.6 all-gather.20.cloned.1.call-done
  294.0 23.2 %all-gather.18.cloned.1.call-done = bf16[1024,1024]{1,0:T(8,128)(2,1)} async-done(((bf16[256,1024]{1,0:T(8,128)(2,1)}), bf16[1024,1024]{1,0:T(8,128)(2,1)}) %all-gather.18.cloned.1.call-update) | async-done | bytes 2097168 | tf_op jit(solution)/shard_map/all_gather | solution.py:159
  317.2 7.4 multiply_convert_fusion.1
  324.6 45.0 %all-gather.22.cloned.1.call-done = bf16[1024,1024]{1,0:T(8,128)(2,1)} async-done(((bf16[1024,128]{1,0:T(8,128)(2,1)}), bf16[1024,1024]{1,0:T(8,128)(2,1)}) %all-gather.22.cloned.1.call-update) | async-done | bytes 2097168 | tf_op jit(solution)/shard_map/all_gather | solution.py:120
  369.6 5.9 convolution_convert_fusion.1
  375.6 29.4 %reduce-scatter.15.cloned.1.call-done = bf16[256,1024]{1,0:T(8,128)(2,1)} async-done(((bf16[1024,1024]{1,0:T(8,128)(2,1)}), bf16[256,1024]{1,0:T(8,128)(2,1)}) %reduce-scatter.15.cloned.1.call-update) | async-done | bytes 524304 | tf_op jit(solution)/shard_map/reduce_scatter | solution.py:163
  408.9 22.7 %all-gather.24.cloned.1.call-done = bf16[1024,1024]{1,0:T(8,128)(2,1)} async-done(((bf16[256,1024]{1,0:T(8,128)(2,1)}), bf16[1024,1024]{1,0:T(8,128)(2,1)}) %all-gather.24.cloned.1.call-update) | async-done | bytes 2097168 | tf_op jit(solution)/shard_map/all_gather | solution.py:178
  431.5 6.6 convert_reduce_fusion
  439.5 3.7 convolution_convert_fusion
  443.3 6.6 fusion.38
  450.1 7.0 fusion.37
  457.2 17.3 %reduce-scatter.17.cloned.1.call-done = bf16[256,1024]{1,0:T(8,128)(2,1)} async-done(((bf16[1024,1024]{1,0:T(8,128)(2,1)}), bf16[256,1024]{1,0:T(8,128)(2,1)}) %reduce-scatter.17.cloned.1.call-update) | async-done | bytes 524304 | tf_op jit(solution)/shard_map/reduce_scatter | solution.py:186
  478.8 3.1 convert_reduce_fusion.4
  485.4 5.5 copy.80
  491.9 3.4 multiply_reduce_fusion
  498.0 2.7 convolution_bitcast_fusion.1
  500.7 5.4 copy.78
  508.7 2.7 convolution_bitcast_fusion.2
  511.4 5.4 copy.76
  517.8 2.7 fusion.29
  521.0 41.5 %all-reduce.17 = (f32[1024]{0:T(1024)S(1)}, f32[1024]{0:T(1024)S(1)}, f32[1024]{0:T(1024)S(1)}, f32[1024]{0:T(1024)S(1)}, f32[1024]{0:T(1024)S(1)}, /*index=5*/f...) all-reduce(f32[1024]{0:T(1024)S(1)} %reduce_sum.186, ...), channel_id=5, replica_groups=mesh['wide'=8,'ffn'=4] {'wide','ffn'}, use_global_device_ids=true, to_apply=%region_15.16.clone | all-reduce | flops 12288 | bytes 98304
  573.8 85.9 %reduce-scatter.21.cloned.1.call-done = f32[128,1024]{1,0:T(8,128)} async-done(((f32[1024,1024]{1,0:T(8,128)}), f32[128,1024]{1,0:T(8,128)}) %reduce-scatter.21.cloned.1.call-update) | async-done | bytes 524304 | tf_op jit(solution)/shard_map/reduce_scatter | solution.py:190
  659.7 145.1 %reduce-scatter.29.cloned.1.call-done = f32[32,1024]{1,0:T(8,128)} async-done(((f32[1024,1024]{1,0:T(8,128)}), f32[32,1024]{1,0:T(8,128)}) %reduce-scatter.29.cloned.1.call-update) | async-done | bytes 131088
  804.8 141.1 %reduce-scatter.27.cloned.1.call-done = f32[32,1024]{1,0:T(8,128)} async-done(((f32[1024,1024]{1,0:T(8,128)}), f32[32,1024]{1,0:T(8,128)}) %reduce-scatter.27.cloned.1.call-update) | async-done | bytes 131088
  945.9 141.2 %reduce-scatter.25.cloned.1.call-done = f32[32,1024]{1,0:T(8,128)} async-done(((f32[1024,1024]{1,0:T(8,128)}), f32[32,1024]{1,0:T(8,128)}) %reduce-scatter.25.cloned.1.call-update) | async-done | bytes 131088
  1087.1 141.3 %reduce-scatter.19.cloned.1.call-done = f32[32,1024]{1,0:T(8,128)} async-done(((f32[1024,1024]{1,0:T(8,128)}), f32[32,1024]{1,0:T(8,128)}) %reduce-scatter.19.cloned.1.call-update) | async-done | bytes 131088 | tf_op jit(solution)/shard_map/reduce_scatter | solution.py:250
  (162 shorter events, 59.0 us)
Async XLA Ops:
  7.2 62.8 %all-gather.12.cloned.1.call-start = ((), (), s32[]{:S(2)}) async-start(), calls=%async_computation.9 | async-start | bytes 2162688 | tf_op jit(solution)/shard_map/all_gather | solution.py:87
  7.9 120.2 %all-gather.14.cloned.1.call-start = ((), (), s32[]{:S(2)}) async-start(), calls=%async_computation.10 | async-start | bytes 2162688 | tf_op jit(solution)/shard_map/all_gather | solution.py:88
  8.7 177.4 %all-gather.10.cloned.1.call-start = ((), (), s32[]{:S(2)}) async-start(), calls=%async_computation.8 | async-start | bytes 2162688 | tf_op jit(solution)/shard_map/all_gather | solution.py:89
  9.4 234.5 %all-gather.16.cloned.1.call-start = ((), (), s32[]{:S(2)}) async-start(), calls=%async_computation.11 | async-start | bytes 2162688 | tf_op jit(solution)/shard_map/all_gather | solution.py:90
  10.0 284.0 %all-gather.20.cloned.1.call-start = ((), (), s32[]{:S(2)}) async-start(), calls=%async_computation.13 | async-start | bytes 2359296 | tf_op jit(solution)/shard_map/all_gather | solution.py:119
  10.6 306.6 %all-gather.18.cloned.1.call-start = ((), (), s32[]{:S(2)}) async-start(), calls=%async_computation.12 | async-start | bytes 2621440 | tf_op jit(solution)/shard_map/all_gather | solution.py:159
  60.4 67.6 %copy-start.2 = (bf16[256,1024]{1,0:T(8,128)(2,1)S(1)}, bf16[256,1024]{1,0:T(8,128)(2,1)}, u32[]{:S(2)}) copy-start(bf16[256,1024]{1,0:T(8,128)(2,1)} %param.18) | copy-start | bytes 1572868
  72.7 115.9 %copy-start.14 = (bf16[256,1024]{0,1:T(8,128)(2,1)}, bf16[256,1024]{0,1:T(8,128)(2,1)S(1)}, u32[]{:S(2)}) copy-start(bf16[256,1024]{0,1:T(8,128)(2,1)S(1)} %copy.62) | copy-start | bytes 1572868
  130.6 58.0 %copy-start.13 = (bf16[256,1024]{0,1:T(8,128)(2,1)}, bf16[256,1024]{0,1:T(8,128)(2,1)S(1)}, u32[]{:S(2)}) copy-start(bf16[256,1024]{0,1:T(8,128)(2,1)S(1)} %copy.63) | copy-start | bytes 1572868
  189.5 1.9 copy-start
  192.3 54.0 %copy-start.22 = (bf16[16,64,256]{2,1,0:T(8,128)(2,1)}, bf16[16,64,256]{2,1,0:T(8,128)(2,1)S(1)}, u32[]{:S(2)}) copy-start(bf16[16,64,256]{2,1,0:T(8,128)(2,1)S(1)} %fusion.23) | copy-start | bytes 1572868
  246.3 2.2 copy-start.24
  247.7 121.9 %all-gather.22.cloned.1.call-start = ((), (), s32[]{:S(2)}) async-start(), calls=%async_computation.14 | async-start | bytes 2359296 | tf_op jit(solution)/shard_map/all_gather | solution.py:120
  248.5 156.6 %reduce-scatter.15.cloned.1.call-start = ((), (), s32[]{:S(2)}) async-start(), calls=%async_computation.15 | async-start | bytes 2621440 | tf_op jit(solution)/shard_map/reduce_scatter | solution.py:163
  375.5 31.3 %copy-start.16 = (bf16[256,1024]{1,0:T(8,128)(2,1)S(1)}, bf16[256,1024]{1,0:T(8,128)(2,1)}, u32[]{:S(2)}) copy-start(bf16[256,1024]{1,0:T(8,128)(2,1)} %param.20) | copy-start | bytes 1572868
  375.5 56.0 %all-gather.24.cloned.1.call-start = ((), (), s32[]{:S(2)}) async-start(), calls=%async_computation.16 | async-start | bytes 2621440 | tf_op jit(solution)/shard_map/all_gather | solution.py:178
  408.8 65.7 %reduce-scatter.17.cloned.1.call-start = ((), (), s32[]{:S(2)}) async-start(), calls=%async_computation.17 | async-start | bytes 2621440 | tf_op jit(solution)/shard_map/reduce_scatter | solution.py:186
  431.5 8.0 copy-start.25
  443.2 130.6 %reduce-scatter.23.cloned.1.call-start = ((), (), s32[]{:S(2)}) async-start(), calls=%async_computation.20 | async-start | bytes 4718592 | tf_op jit(solution)/shard_map/reduce_scatter | solution.py:191
  449.9 209.9 %reduce-scatter.21.cloned.1.call-start = ((), (), s32[]{:S(2)}) async-start(), calls=%async_computation.19 | async-start | bytes 4718592 | tf_op jit(solution)/shard_map/reduce_scatter | solution.py:190
  457.1 347.7 %reduce-scatter.29.cloned.1.call-start = ((), (), s32[]{:S(2)}) async-start(), calls=%async_computation.23 | async-start | bytes 4325376
  474.5 1.7 copy-start.21
  478.8 3.9 copy-start.3
  490.9 455.0 %reduce-scatter.27.cloned.1.call-start = ((), (), s32[]{:S(2)}) async-start(), calls=%async_computation.22 | async-start | bytes 4325376
  491.9 3.5 copy-start.1
  506.1 580.9 %reduce-scatter.25.cloned.1.call-start = ((), (), s32[]{:S(2)}) async-start(), calls=%async_computation.21 | async-start | bytes 4325376
  506.2 2.5 copy-start.5
  516.8 711.6 %reduce-scatter.19.cloned.1.call-start = ((), (), s32[]{:S(2)}) async-start(), calls=%async_computation.18 | async-start | bytes 4325376 | tf_op jit(solution)/shard_map/reduce_scatter | solution.py:250
  520.5 47.3 %copy-start.12 = (bf16[16,64,256]{2,1,0:T(8,128)(2,1)S(1)}, bf16[16,64,256]{2,1,0:T(8,128)(2,1)}, u32[]{:S(2)}) copy-start(bf16[16,64,256]{2,1,0:T(8,128)(2,1)} %copy-done.11) | copy-start | bytes 1572868
  567.8 2.5 copy-start.10
  567.8 2.5 copy-start.19
  570.3 1.8 copy-start.20
  (11 other events, 12.6 us)
Sparse Core Ops, SparseCore 0:
  10.9 59.1 all-gather.11
  72.9 55.1 all-gather.13
  131.0 55.0 all-gather.9
  188.8 55.0 all-gather.15
  245.9 48.0 all-gather.19
  296.0 21.1 all-gather.17
  319.2 50.3 all-gather.21
  375.6 29.3 reduce-scatter.14
  408.9 22.5 all-gather.23
  443.4 31.1 reduce-scatter.16
  478.7 89.1 reduce-scatter.22
  572.0 87.6 reduce-scatter.20
  662.6 142.1 reduce-scatter.28
  807.5 138.3 reduce-scatter.26
  948.6 138.4 reduce-scatter.24
  1089.8 138.5 reduce-scatter.18
where the time goes:
time: 1240 us; the launch traced here: 1230 us
  waiting for transfers between devices  974 us (79%)
  blocking collectives  124 us (10%)
  matrix products  73.8 us (6%)
  local copies, waits for them, and re-layouts  38.8 us (3%)
  between operations  14.5 us (1%)
    unnamed x19, waiting for transfers between devices  431 us
    reduce_scatter x1, waiting for transfers between devices, body(): lax.psum_scatter(grad_output_w, ('wide', 'ffn'), scatter_dimension=0, til...  141 us
    reduce_scatter x1, waiting for transfers between devices, body(): lax.psum_scatter(grad_up_w, 'wide', scatter_dimension=0, tiled=True)  85.9 us
    unnamed x2, blocking collectives  83.8 us
    all_gather x1, waiting for transfers between devices, body(): lax.all_gather(w_value, ('wide', 'ffn'), axis=0, tiled=True)  55.5 us
    all_gather x1, waiting for transfers between devices, body(): lax.all_gather(w_key, ('wide', 'ffn'), axis=0, tiled=True)  55.4 us
    all_gather x1, waiting for transfers between devices, body(): lax.all_gather(w_output, ('wide', 'ffn'), axis=0, tiled=True)  51.6 us
    all_gather x1, waiting for transfers between devices, body(): lax.all_gather(w_down, 'wide', axis=1, tiled=True)  45 us
  transfers between devices with their start and end apart: 16, of which 15 were waited for; matrix products, arithmetic and copies ran while one was open for 8% of the time, Pallas kernels for 0%

commit v1 on v0

--- a/solution.py
+++ b/solution.py
@@ -1,3 +1,4 @@
+import functools
 import math
 import jax
 import jax.numpy as jnp
@@ -8,6 +9,31 @@
 HEADS = 16
 HEAD_DIM = 64
 norm_eps = 1e-12
+
+
+def mark_the_axis_part(base_x, ax_name):
+    moved = lax.axis_size(ax_name)
+    x_now, seen_now, res = (moved, lax.axis_index(ax_name), base_x.shape[1])
+    vals = [(i0, (i0 + 1) % x_now) for i0 in range(x_now)]
+    work_now = jnp.zeros((*base_x.shape[:1], x_now * res, *base_x.shape[2:]), base_x.dtype)
+    work_now = lax.dynamic_update_slice_in_dim(work_now, base_x, seen_now * res, axis=1)
+    before = step_out = base_x
+    store = [(i0, (i0 - 1) % x_now) for i0 in range(x_now)]
+    current_block = x_now // 2
+    for dd in range(1, current_block + 1):
+        before = lax.ppermute(before, ax_name, perm=vals)
+        work_now = lax.dynamic_update_slice_in_dim(
+            work_now, before, (seen_now - dd) % x_now * res, axis=1
+        )
+        if dd < x_now - current_block:
+            step_out = lax.ppermute(step_out, ax_name, perm=store)
+            work_now = lax.dynamic_update_slice_in_dim(
+                work_now, step_out, (seen_now + dd) % x_now * res, axis=1
+            )
+    return work_now
+
+
+fill_circles = functools.partial(mark_the_axis_part, ax_name="wide")
 
 
 def matmul(left, right):
@@ -115,10 +141,7 @@
         gain_two,
         shift_two,
     ) = [vector.astype(jnp.float32) for vector in gathered[4:]]
-    up_part, down_part = (
-        lax.all_gather(w_up, "wide", axis=0, tiled=True),
-        lax.all_gather(w_down, "wide", axis=1, tiled=True),
-    )
+    up_part, down_part = (lax.all_gather(w_up, "wide", axis=0, tiled=True), fill_circles(w_down))
     row_count = hidden_in.shape[0]
     score_scale = HEAD_DIM ** (-0.5)
     residual_in = hidden_in.astype(jnp.float32)

time: 1240 us -> 1210 us (0.976)
  waiting for transfers between devices: 974 us -> 920 us
  starting transfers between devices: 0.86 us -> 18 us
    all_gather x1 -> x0, waiting for transfers between devices: 45 us -> none  [body(): lax.all_gather(w_down, 'wide', axis=1, tiled=True)]
    all_gather x1, waiting for transfers between devices: 23.2 us -> 0.01 us  [body(): group_rows = lax.all_gather(normed_low, 'ffn', axis=0, tiled=True)]
    ppermute x0 -> x7, waiting for transfers between devices: none -> 22.2 us  [the longest x4 22.2 us: mark_the_axis_part(): before = lax.ppermute(before, ax_name, perm=vals)]
    ppermute x0 -> x7, starting transfers between devices: none -> 17.2 us  [the longest x3 10.3 us: mark_the_axis_part(): step_out = lax.ppermute(step_out, ax_name, perm=store)]
    unnamed x19 -> x18, waiting for transfers between devices: 431 us -> 429 us
    unnamed x82 -> x86, local copies, waits for them, and re-layouts: 37.5 us -> 37.6 us
  transfers between devices with their start and end apart: 16 -> 22, of which waited for: 15 -> 15; matrix products, arithmetic and copies ran while one was open for 8% -> 8% of each run, Pallas kernels for 0% -> 0%
where the time goes in v1:
time: 1210 us; the launch traced here: 1200 us
  waiting for transfers between devices  920 us (76%)
  blocking collectives  123 us (10%)
  matrix products  72.4 us (6%)
  local copies, waits for them, and re-layouts  46.4 us (4%)
  starting transfers between devices  18 us (1%)
  between operations  14.8 us (1%)
    unnamed x18, waiting for transfers between devices  429 us
    reduce_scatter x1, waiting for transfers between devices, body(): lax.psum_scatter(grad_output_w, ('wide', 'ffn'), scatter_dimension=0, til...  141 us
    reduce_scatter x1, waiting for transfers between devices, body(): lax.psum_scatter(grad_up_w, 'wide', scatter_dimension=0, tiled=True)  87.8 us
    unnamed x2, blocking collectives  83.4 us
    all_gather x1, waiting for transfers between devices, body(): lax.all_gather(w_value, ('wide', 'ffn'), axis=0, tiled=True)  55.5 us
    all_gather x1, waiting for transfers between devices, body(): lax.all_gather(w_key, ('wide', 'ffn'), axis=0, tiled=True)  55.4 us
    all_gather x1, waiting for transfers between devices, body(): lax.all_gather(w_output, ('wide', 'ffn'), axis=0, tiled=True)  51.6 us
    all_gather x1, blocking collectives, body(): lax.all_gather(b_up, ('wide', 'ffn'), axis=0, tiled=True)  39.6 us
  transfers between devices with their start and end apart: 22, of which 15 were waited for; matrix products, arithmetic and copies ran while one was open for 8% of the time, Pallas kernels for 0%

profile of v1, /device:TPU:0, one launch (start us, length us, event | category | flops | bytes accessed | tf_op | source)
XLA Modules:
  0.0 1204.1 jit_solution(4756584306294160066)
XLA Ops:
  17.3 42.2 %all-reduce.18 = (bf16[1024]{0:T(1024)(128)(2,1)S(1)}, bf16[1024]{0:T(1024)(128)(2,1)S(1)}, bf16[1024]{0:T(1024)(128)(2,1)S(1)}, bf16[1024]{0:T(1024)(128)(2,1)S...) all-reduce(bf16[1024]{0:T(1024)(128)(2,1)S(1)} %dynamic-update-slic, ...), channel_id=1, replica_groups=mesh['wide'=8,'ffn'=4] {'wide','ffn'}, use_global_device_ids=true, to_apply=%add | all-reduce | flops 8192 | bytes 32768
  60.5 9.6 all-gather.11.cloned.1.call-done
  72.7 55.4 %all-gather.13.cloned.1.call-done = bf16[1024,1024]{1,0:T(8,128)(2,1)} async-done(((bf16[32,1024]{1,0:T(8,128)(2,1)}), bf16[1024,1024]{1,0:T(8,128)(2,1)}) %all-gather.13.cloned.1.call-update) | async-done | bytes 2097168 | tf_op jit(solution)/shard_map/all_gather | solution.py:114
  130.6 55.5 %all-gather.9.cloned.1.call-done = bf16[1024,1024]{1,0:T(8,128)(2,1)} async-done(((bf16[32,1024]{1,0:T(8,128)(2,1)}), bf16[1024,1024]{1,0:T(8,128)(2,1)}) %all-gather.9.cloned.1.call-update) | async-done | bytes 2097168 | tf_op jit(solution)/shard_map/all_gather | solution.py:115
  192.3 51.6 %all-gather.15.cloned.1.call-done = bf16[1024,1024]{1,0:T(8,128)(2,1)} async-done(((bf16[32,1024]{1,0:T(8,128)(2,1)}), bf16[1024,1024]{1,0:T(8,128)(2,1)}) %all-gather.15.cloned.1.call-update) | async-done | bytes 2097168 | tf_op jit(solution)/shard_map/all_gather | solution.py:116
  249.3 3.3 collective-permute-start.1
  252.6 11.1 collective-permute-done
  270.7 39.6 %all-gather = bf16[32,1,128]{2,1,0:T(2,128)(2,1)S(1)} all-gather(bf16[1,1,128]{2,1,0:T(2,128)(2,1)S(1)} %bitcast.90), channel_id=1, replica_groups=mesh['wide'=8,'ffn'=4] {'wide','ffn'}, dimensions={0}, use_global_device_ids=true | all-gather | bytes 8448 | tf_op jit(solution)/shard_map/all_gather | solution.py:122
  312.0 4.8 collective-permute-start.5
  317.5 5.0 collective-permute-done.4
  322.5 2.9 collective-permute-start.6
  327.7 6.2 collective-permute-done.6
  334.6 6.8 multiply_convert_fusion.1
  342.7 5.3 convolution_convert_fusion.1
  348.1 27.1 %reduce-scatter.15.cloned.1.call-done = bf16[256,1024]{1,0:T(8,128)(2,1)} async-done(((bf16[1024,1024]{1,0:T(8,128)(2,1)}), bf16[256,1024]{1,0:T(8,128)(2,1)}) %reduce-scatter.15.cloned.1.call-update) | async-done | bytes 524304 | tf_op jit(solution)/shard_map/reduce_scatter | solution.py:186
  379.0 22.6 %all-gather.21.cloned.1.call-done = bf16[1024,1024]{1,0:T(8,128)(2,1)} async-done(((bf16[256,1024]{1,0:T(8,128)(2,1)}), bf16[1024,1024]{1,0:T(8,128)(2,1)}) %all-gather.21.cloned.1.call-update) | async-done | bytes 2097168 | tf_op jit(solution)/shard_map/all_gather | solution.py:201
  401.7 6.6 convert_reduce_fusion
  409.6 3.7 convolution_convert_fusion
  413.4 6.6 fusion.38
  420.2 7.0 fusion.37
  427.3 17.4 %reduce-scatter.17.cloned.1.call-done = bf16[256,1024]{1,0:T(8,128)(2,1)} async-done(((bf16[1024,1024]{1,0:T(8,128)(2,1)}), bf16[256,1024]{1,0:T(8,128)(2,1)}) %reduce-scatter.17.cloned.1.call-update) | async-done | bytes 524304 | tf_op jit(solution)/shard_map/reduce_scatter | solution.py:209
  449.3 3.0 convert_reduce_fusion.4
  455.0 5.7 copy.80
  461.7 3.4 multiply_reduce_fusion
  470.0 5.4 copy.78
  479.8 5.4 copy.76
  489.8 41.1 %all-reduce.17 = (f32[1024]{0:T(1024)S(1)}, f32[1024]{0:T(1024)S(1)}, f32[1024]{0:T(1024)S(1)}, f32[1024]{0:T(1024)S(1)}, f32[1024]{0:T(1024)S(1)}, /*index=5*/f...) all-reduce(f32[1024]{0:T(1024)S(1)} %reduce_sum.186, ...), channel_id=5, replica_groups=mesh['wide'=8,'ffn'=4] {'wide','ffn'}, use_global_device_ids=true, to_apply=%region_15.16.clone | all-reduce | flops 12288 | bytes 98304
  542.2 87.8 %reduce-scatter.21.cloned.1.call-done = f32[128,1024]{1,0:T(8,128)} async-done(((f32[1024,1024]{1,0:T(8,128)}), f32[128,1024]{1,0:T(8,128)}) %reduce-scatter.21.cloned.1.call-update) | async-done | bytes 524304 | tf_op jit(solution)/shard_map/reduce_scatter | solution.py:213
  630.1 144.2 %reduce-scatter.29.cloned.1.call-done = f32[32,1024]{1,0:T(8,128)} async-done(((f32[1024,1024]{1,0:T(8,128)}), f32[32,1024]{1,0:T(8,128)}) %reduce-scatter.29.cloned.1.call-update) | async-done | bytes 131088
  774.3 141.2 %reduce-scatter.27.cloned.1.call-done = f32[32,1024]{1,0:T(8,128)} async-done(((f32[1024,1024]{1,0:T(8,128)}), f32[32,1024]{1,0:T(8,128)}) %reduce-scatter.27.cloned.1.call-update) | async-done | bytes 131088
  915.5 140.8 %reduce-scatter.25.cloned.1.call-done = f32[32,1024]{1,0:T(8,128)} async-done(((f32[1024,1024]{1,0:T(8,128)}), f32[32,1024]{1,0:T(8,128)}) %reduce-scatter.25.cloned.1.call-update) | async-done | bytes 131088
  1056.3 141.1 %reduce-scatter.19.cloned.1.call-done = f32[32,1024]{1,0:T(8,128)} async-done(((f32[1024,1024]{1,0:T(8,128)}), f32[32,1024]{1,0:T(8,128)}) %reduce-scatter.19.cloned.1.call-update) | async-done | bytes 131088 | tf_op jit(solution)/shard_map/reduce_scatter | solution.py:273
  (186 shorter events, 80.0 us)
Async XLA Ops:
  7.2 62.8 %all-gather.11.cloned.1.call-start = ((), (), s32[]{:S(2)}) async-start(), calls=%async_computation.9 | async-start | bytes 2162688 | tf_op jit(solution)/shard_map/all_gather | solution.py:113
  7.9 120.2 %all-gather.13.cloned.1.call-start = ((), (), s32[]{:S(2)}) async-start(), calls=%async_computation.10 | async-start | bytes 2162688 | tf_op jit(solution)/shard_map/all_gather | solution.py:114
  8.7 177.4 %all-gather.9.cloned.1.call-start = ((), (), s32[]{:S(2)}) async-start(), calls=%async_computation.8 | async-start | bytes 2162688 | tf_op jit(solution)/shard_map/all_gather | solution.py:115
  9.4 234.5 %all-gather.15.cloned.1.call-start = ((), (), s32[]{:S(2)}) async-start(), calls=%async_computation.11 | async-start | bytes 2162688 | tf_op jit(solution)/shard_map/all_gather | solution.py:116
  10.0 324.6 %all-gather.19.cloned.1.call-start = ((), (), s32[]{:S(2)}) async-start(), calls=%async_computation.13 | async-start | bytes 2359296 | tf_op jit(solution)/shard_map/all_gather | solution.py:144
  10.6 324.0 %all-gather.17.cloned.1.call-start = ((), (), s32[]{:S(2)}) async-start(), calls=%async_computation.12 | async-start | bytes 2621440 | tf_op jit(solution)/shard_map/all_gather | solution.py:182
  60.4 67.7 %copy-start.4 = (bf16[256,1024]{1,0:T(8,128)(2,1)S(1)}, bf16[256,1024]{1,0:T(8,128)(2,1)}, u32[]{:S(2)}) copy-start(bf16[256,1024]{1,0:T(8,128)(2,1)} %param.18) | copy-start | bytes 1572868
  72.7 115.9 %copy-start.14 = (bf16[256,1024]{0,1:T(8,128)(2,1)}, bf16[256,1024]{0,1:T(8,128)(2,1)S(1)}, u32[]{:S(2)}) copy-start(bf16[256,1024]{0,1:T(8,128)(2,1)S(1)} %copy.62) | copy-start | bytes 1572868
  130.6 58.0 %copy-start.13 = (bf16[256,1024]{0,1:T(8,128)(2,1)}, bf16[256,1024]{0,1:T(8,128)(2,1)S(1)}, u32[]{:S(2)}) copy-start(bf16[256,1024]{0,1:T(8,128)(2,1)S(1)} %copy.63) | copy-start | bytes 1572868
  192.3 54.0 %copy-start.22 = (bf16[16,64,256]{2,1,0:T(8,128)(2,1)}, bf16[16,64,256]{2,1,0:T(8,128)(2,1)S(1)}, u32[]{:S(2)}) copy-start(bf16[16,64,256]{2,1,0:T(8,128)(2,1)S(1)} %fusion.23) | copy-start | bytes 1572868
  246.7 24.1 %copy-start.25 = (bf16[128]{0:T(256)(128)(2,1)S(1)}, bf16[128]{0:T(256)(128)(2,1)}, u32[]{:S(2)}) copy-start(bf16[128]{0:T(256)(128)(2,1)} %param.31) | copy-start | bytes 772
  247.7 127.4 %reduce-scatter.15.cloned.1.call-start = ((), (), s32[]{:S(2)}) async-start(), calls=%async_computation.14 | async-start | bytes 2621440 | tf_op jit(solution)/shard_map/reduce_scatter | solution.py:186
  247.8 15.9 %collective-permute-start = (bf16[1024,128]{1,0:T(8,128)(2,1)S(1)}, bf16[1024,128]{1,0:T(8,128)(2,1)S(1)}, u32[]{:S(2)}, u32[]{:S(2)}) collective-permute-start(bf16[1024,128]{1,0:T(8,128)(2,1)S(1)} %copy-done.24), channel_id=1, source_target_pairs={{0,4},{4,8},{8,12},{12,16},{16,20},{20,24},{24,28},{28,0},{1,5},{5... | collective-permute-start | bytes 786440 | tf_op jit(solution)/shard_map/ppermute | solution.py:24
  249.3 16.9 %collective-permute-start.1 = (bf16[1024,128]{1,0:T(8,128)(2,1)S(1)}, bf16[1024,128]{1,0:T(8,128)(2,1)S(1)}, u32[]{:S(2)}, u32[]{:S(2)}) collective-permute-start(bf16[1024,128]{1,0:T(8,128)(2,1)S(1)} %copy-done.24), channel_id=1, source_target_pairs={{0,28},{4,0},{8,4},{12,8},{16,12},{20,16},{24,20},{28,24},{1,29},{... | collective-permute-start | bytes 786440 | tf_op jit(solution)/shard_map/ppermute | solution.py:29
  263.7 46.8 %collective-permute-start.2 = (bf16[1024,128]{1,0:T(8,128)(2,1)S(1)}, bf16[1024,128]{1,0:T(8,128)(2,1)S(1)}, u32[]{:S(2)}, u32[]{:S(2)}) collective-permute-start(bf16[1024,128]{1,0:T(8,128)(2,1)S(1)} %collective-permute-done), channel_id=1, source_target_pairs={{0,4},{4,8},{8,12},{12,16},{16,20},{20,24},{24,28},{28,0},{1,5},{5... | collective-permute-start | bytes 786440 | tf_op jit(solution)/shard_map/ppermute | solution.py:24
  266.1 45.8 %collective-permute-start.3 = (bf16[1024,128]{1,0:T(8,128)(2,1)S(1)}, bf16[1024,128]{1,0:T(8,128)(2,1)S(1)}, u32[]{:S(2)}, u32[]{:S(2)}) collective-permute-start(bf16[1024,128]{1,0:T(8,128)(2,1)S(1)} %collective-permute-done.1), channel_id=1, source_target_pairs={{0,28},{4,0},{8,4},{12,8},{16,12},{20,16},{24,20},{28,24},{1,29},{... | collective-permute-start | bytes 786440 | tf_op jit(solution)/shard_map/ppermute | solution.py:29
  310.5 12.0 collective-permute-start.4
  312.0 14.9 %collective-permute-start.5 = (bf16[1024,128]{1,0:T(8,128)(2,1)S(1)}, bf16[1024,128]{1,0:T(8,128)(2,1)S(1)}, u32[]{:S(2)}, u32[]{:S(2)}) collective-permute-start(bf16[1024,128]{1,0:T(8,128)(2,1)S(1)} %collective-permute-done.3), channel_id=1, source_target_pairs={{0,28},{4,0},{8,4},{12,8},{16,12},{20,16},{24,20},{28,24},{1,29},{... | collective-permute-start | bytes 786440 | tf_op jit(solution)/shard_map/ppermute | solution.py:29
  322.5 11.4 collective-permute-start.6
  348.0 28.9 %copy-start.16 = (bf16[256,1024]{1,0:T(8,128)(2,1)S(1)}, bf16[256,1024]{1,0:T(8,128)(2,1)}, u32[]{:S(2)}) copy-start(bf16[256,1024]{1,0:T(8,128)(2,1)} %param.20) | copy-start | bytes 1572868
  348.0 53.7 %all-gather.21.cloned.1.call-start = ((), (), s32[]{:S(2)}) async-start(), calls=%async_computation.15 | async-start | bytes 2621440 | tf_op jit(solution)/shard_map/all_gather | solution.py:201
  379.0 65.7 %reduce-scatter.17.cloned.1.call-start = ((), (), s32[]{:S(2)}) async-start(), calls=%async_computation.16 | async-start | bytes 2621440 | tf_op jit(solution)/shard_map/reduce_scatter | solution.py:209
  401.7 8.0 copy-start.26
  413.4 128.9 %reduce-scatter.23.cloned.1.call-start = ((), (), s32[]{:S(2)}) async-start(), calls=%async_computation.19 | async-start | bytes 4718592 | tf_op jit(solution)/shard_map/reduce_scatter | solution.py:214
  420.0 210.1 %reduce-scatter.21.cloned.1.call-start = ((), (), s32[]{:S(2)}) async-start(), calls=%async_computation.18 | async-start | bytes 4718592 | tf_op jit(solution)/shard_map/reduce_scatter | solution.py:213
  427.2 347.1 %reduce-scatter.29.cloned.1.call-start = ((), (), s32[]{:S(2)}) async-start(), calls=%async_computation.22 | async-start | bytes 4325376
  460.7 454.8 %reduce-scatter.27.cloned.1.call-start = ((), (), s32[]{:S(2)}) async-start(), calls=%async_computation.21 | async-start | bytes 4325376
  461.7 3.5 copy-start.1
  467.0 2.9 copy-start.9
  475.4 580.9 %reduce-scatter.25.cloned.1.call-start = ((), (), s32[]{:S(2)}) async-start(), calls=%async_computation.20 | async-start | bytes 4325376
  485.3 712.1 %reduce-scatter.19.cloned.1.call-start = ((), (), s32[]{:S(2)}) async-start(), calls=%async_computation.17 | async-start | bytes 4325376 | tf_op jit(solution)/shard_map/reduce_scatter | solution.py:273
  489.3 46.9 %copy-start.12 = (bf16[16,64,256]{2,1,0:T(8,128)(2,1)S(1)}, bf16[16,64,256]{2,1,0:T(8,128)(2,1)}, u32[]{:S(2)}) copy-start(bf16[16,64,256]{2,1,0:T(8,128)(2,1)} %copy-done.11) | copy-start | bytes 1572868
  (19 other events, 31.1 us)
Sparse Core Ops, SparseCore 0:
  10.9 59.1 all-gather.10
  72.9 55.1 all-gather.12
  131.0 55.0 all-gather.8
  188.8 55.0 all-gather.14
  245.9 55.9 all-gather.18
  303.9 21.0 all-gather.16
  348.1 27.0 reduce-scatter.14
  379.1 22.5 all-gather.20
  413.5 31.1 reduce-scatter.16
  448.7 89.0 reduce-scatter.22
  542.1 87.9 reduce-scatter.20
  632.8 141.4 reduce-scatter.28
  777.2 138.2 reduce-scatter.26
  918.2 138.0 reduce-scatter.24
  1059.0 138.3 reduce-scatter.18
